TPU v7x, 256 devices: a whole 4x4x8 slice. The times are simulated.
256 devices in a mesh: dp: 32 (over y, z), vocab: 8 (over x, core).
Axes of the slice: x: 4, y: 4, z: 8, core: 2. Of those that a mesh axis runs over, the one named last changes fastest.
Arguments:
- hidden: bfloat16 [12288, 4096], P('dp'), may hold values from -6 to 6
- head_weight: bfloat16 [4096, 16000], P('dp', 'vocab'), may hold values from -0.09375 to 0.09375
- head_bias: float32 [16000], P('vocab'), may hold values from -3.5 to -1.5
- query_len: int32 [128], P('dp'), may hold values from 8 to 32
- passage_len: int32 [128], P('dp'), may hold values from 16 to 64
- neg_owner: int32 [128, 8], P('dp'), may hold values from 0 to 31, all different within a row; in each aligned block of 4 rows (0 to 3, 4 to 7, ...) at most 2 rows name the same one
- neg_index: int32 [128, 8], P('dp'), may hold values from 0 to 3
- teacher: float32 [128, 8], P('dp'), may hold values from -8 to 8
Outputs:
- margin_error: float32 [128, 8], P('dp')
- hidden_grad: float32 [12288, 4096], P(('dp', 'vocab'))
Inputs may be any that keep to these rules, and one draw needn't show every extreme that they name: `neg_owner`: the 8 negatives of a query have different holders. Among the queries of one index of dp no holder appears more than 2 times, and in some of those blocks one holder appears exactly 2 times.
All inputs are finite; a program needn't handle non-finite values.
Results may differ from a plain program's by a relative error of at most 0.0028.
Values may be sent and summed in bfloat16 or wider, within the bound.
A program may use at most 128 MiB of HBM per device.

v0:
```python
import jax
import jax.numpy as jnp
from jax import lax
from jax.sharding import PartitionSpec as P

LQ = 32
LP = 64
TAU = 0.05


def soft_pool(token_logits, token_mask):
    activation = jnp.log1p(jnp.maximum(token_logits, 0.0))
    weights = jnp.exp(activation / TAU) * token_mask[:, :, None]
    summed = jnp.sum(weights, axis=1)
    valid_count = jnp.sum(token_mask, axis=1)[:, None]
    return (TAU * jnp.log(summed / valid_count), weights / summed[:, None, :])


def lengths_mask(lengths, span):
    return (jnp.arange(span)[None, :] < lengths[:, None]).astype(jnp.float32)


def per_device(
    hidden, head_weight, head_bias, query_len, passage_len, neg_owner, neg_index, teacher
):
    query_count = neg_owner.shape[0]
    neg_count = neg_owner.shape[1]
    owners = lax.axis_size("dp")
    head_full = lax.all_gather(head_weight, "dp", axis=0, tiled=True)
    vocab_width = head_full.shape[1]
    logits = jnp.dot(hidden, head_full, preferred_element_type=jnp.float32) + head_bias[None, :]
    query_tokens = query_count * LQ
    query_rep, query_weights = soft_pool(
        logits[:query_tokens].reshape(query_count, LQ, vocab_width), lengths_mask(query_len, LQ)
    )
    passage_rep, passage_weights = soft_pool(
        logits[query_tokens:].reshape(query_count, LP, vocab_width), lengths_mask(passage_len, LP)
    )
    gathered = lax.all_gather(passage_rep, "dp", axis=0, tiled=True)
    passage_ids = neg_owner * query_count + neg_index
    neg_rows = jnp.take(gathered, passage_ids.reshape(-1), axis=0).reshape(
        query_count, neg_count, vocab_width
    )
    pos_part = jnp.sum(query_rep * passage_rep, axis=1)
    neg_part = jnp.sum(query_rep[:, None, :] * neg_rows, axis=2)
    positive, negative = lax.psum((pos_part, neg_part), "vocab")
    margin_error = positive[:, None] - negative - teacher
    grad_pos = jnp.sum(margin_error, axis=1)
    grad_neg = -margin_error
    query_grad = grad_pos[:, None] * passage_rep + jnp.sum(grad_neg[:, :, None] * neg_rows, axis=1)
    neg_terms = (grad_neg[:, :, None] * query_rep[:, None, :]).reshape(-1, vocab_width)
    scattered = jax.ops.segment_sum(
        neg_terms, passage_ids.reshape(-1), num_segments=owners * query_count
    )
    returned_grad = lax.psum_scatter(scattered, "dp", scatter_dimension=0, tiled=True)
    passage_grad = grad_pos[:, None] * query_rep + returned_grad
    relu_slope = (logits > 0).astype(jnp.float32) / (1.0 + jnp.maximum(logits, 0.0))
    d_query = (query_grad[:, None, :] * query_weights).reshape(-1, vocab_width)
    d_passage = (passage_grad[:, None, :] * passage_weights).reshape(-1, vocab_width)
    logit_grad = (jnp.concatenate([d_query, d_passage], axis=0) * relu_slope).astype(jnp.bfloat16)
    hidden_grad = lax.psum_scatter(
        lax.dot_general(
            logit_grad, head_full, (((1,), (1,)), ((), ())), preferred_element_type=jnp.float32
        ),
        "vocab",
        scatter_dimension=0,
        tiled=True,
    )
    return (margin_error, hidden_grad)


def solution(mesh):
    return jax.shard_map(
        per_device,
        mesh=mesh,
        in_specs=(
            P("dp", None),
            P("dp", "vocab"),
            P("vocab"),
            P("dp"),
            P("dp"),
            P("dp", None),
            P("dp", None),
            P("dp", None),
        ),
        out_specs=(P("dp", None), P(("dp", "vocab"), None)),
        check_vma=False,
    )
```

profile of v0, /device:TPU:1, one launch (start us, length us, event | category | flops | bytes accessed | tf_op | source)
XLA Modules:
  0.0 486.5 jit_solution(886235719207810661)
XLA Ops:
  7.2 0.7 all-gather.3.cloned.1.call-update
  8.0 0.9 compare_and_fusion
  8.8 0.1 reshape.191
  8.9 0.7 reshape.204
  9.6 0.6 broadcast_in_dim.13
  10.2 0.8 fusion.22
  11.0 0.8 fusion.21
  11.9 0.7 fusion.18
  12.6 0.7 fusion.19
  13.3 144.3 %all-gather.3.cloned.1.call-done = bf16[4096,2000]{0,1:T(8,128)(2,1)} async-done(((bf16[128,2000]{0,1:T(8,128)(2,1)}), bf16[4096,2000]{0,1:T(8,128)(2,1)}) %all-gather.3.cloned.1.call-update) | async-done | bytes 16384016 | tf_op jit(solution)/shard_map/all_gather | solution.py:29
  157.6 12.0 %convolution_add_fusion = f32[384,2000]{0,1:T(8,128)S(1)} fusion(bf16[384,4096]{1,0:T(8,128)(2,1)S(1)} %copy-done, bf16[4096,2000]{0,1:T(8,128)(2,1)} %all-gather.3.cloned.1.call-done, f32[2000]{0:T(1024)} %param.10), kind=kOutput, calls=%fused_computation.4 | convolution fusion | flops 6292224000 | bytes 22609728 | tf_op jit(solution)/shard_map/dot_general | solution.py:31
  169.6 1.7 fusion.10
  171.3 0.2 copy-done.1
  171.5 2.2 fusion.3
  173.7 2.6 copy.18
  176.3 2.9 copy.19
  179.2 1.4 multiply_reduce_fusion.1
  180.6 1.9 multiply_reduce_fusion
  182.5 0.2 multiply_reduce_fusion.2
  182.7 0.6 copy-done.3
  183.3 42.1 %all-gather = f32[32,4,2000]{2,1,0:T(4,128)} all-gather(f32[1,4,2000]{2,1,0:T(4,128)S(1)} %multiply_bitcast_fusion), channel_id=1, replica_groups=mesh['dp'=32,'vocab'=8] {'dp'}, dimensions={0}, use_global_device_ids=true | all-gather | bytes 1056000 | tf_op jit(solution)/shard_map/all_gather | solution.py:39
  225.4 2.6 reshape.212
  228.0 2.0 gather_fusion
  230.0 1.5 fusion.13
  231.4 0.8 reduce_sum.80
  232.2 27.3 %all-reduce.1 = (f32[4,8]{1,0:T(4,128)}, f32[4]{0:T(128)}) all-reduce(f32[4,8]{1,0:T(4,128)S(1)} %reduce_sum.80, f32[4]{0:T(128)S(1)} %get-tuple-element.6), channel_id=1, replica_groups=mesh['dp'=32,'vocab'=8] {'vocab'}, use_global_device_ids=true, to_apply=%region_7.8 | all-reduce | flops 36 | bytes 288 | tf_op jit(solution)/shard_map/psum | solution.py:46
  259.4 1.5 fusion.26
  260.9 0.7 mul.151
  261.6 2.2 scatter_custom_fusion
  263.8 0.2 reduce-scatter.2.cloned.1.call-start
  264.0 0.7 reshape.192
  264.8 1.3 dynamic-slice
  266.7 1.1 div.69
  267.8 2.6 copy.20
  270.4 1.7 div.72
  272.1 3.0 copy.23
  275.1 0.2 fusion.15
  275.2 130.2 %all-reduce.4.cloned.1.call-done = f32[128,2000]{1,0:T(8,128)} async-done(((f32[128,2000]{1,0:T(8,128)}), f32[128,2000]{1,0:T(8,128)}) %all-reduce.4.cloned.1.call-update) | async-done | bytes 1024016
  405.4 0.9 multiply_add_fusion
  406.3 1.1 mul.145
  407.4 2.6 copy.21
  410.1 1.6 mul.154
  411.7 2.9 copy.24
  414.6 2.6 divide_multiply_fusion.1
  417.1 0.3 copy-done.2
  417.4 3.3 divide_multiply_fusion
  420.7 12.6 %fusion.4 = f32[384,4096]{1,0:T(8,128)} fusion(bf16[4096,2000]{0,1:T(8,128)(2,1)} %all-gather.3.cloned.1.call-done, f32[256,2000]{0,1:T(8,128)S(1)} %divide_multiply_fusion, f32[128,2000]{0,1:T(8,128)S(1)} %divide_multiply_fusion.1, f32[384,2000]{0,1:T(8,128)S(1)} %copy-done.2), kind=kOutput, calls=%fused_computation.11 | convolution fusion | flops 6297600000 | bytes 28819456 | tf_op jit(solution)/shard_map/dot_general | solution.py:62
  433.4 46.6 %reduce-scatter.2.cloned.1.call-done = f32[48,4096]{1,0:T(8,128)} async-done(((f32[384,4096]{1,0:T(8,128)}), f32[48,4096]{1,0:T(8,128)}) %reduce-scatter.2.cloned.1.call-update) | async-done | bytes 786448 | tf_op jit(solution)/shard_map/reduce_scatter | solution.py:61
  (28 shorter events, 0.3 us)
Async XLA Ops:
  7.2 150.4 %copy-start = (bf16[384,4096]{1,0:T(8,128)(2,1)S(1)}, bf16[384,4096]{1,0:T(8,128)(2,1)}, u32[]{:S(2)}) copy-start(bf16[384,4096]{1,0:T(8,128)(2,1)} %param.8) | copy-start | bytes 9437188
  7.2 150.4 %all-gather.3.cloned.1.call-start = ((), (), s32[]{:S(2)}) async-start(), calls=%async_computation.1 | async-start | bytes 16896000 | tf_op jit(solution)/shard_map/all_gather | solution.py:29
  7.9 397.5 %all-reduce.4.cloned.1.call-start = ((), (), s32[]{:S(2)}) async-start(), calls=%async_computation.3 | async-start | bytes 2097152
  8.8 160.8 %copy-start.7 = (pred[4,8]{1,0:T(4,128)(4,1)}, pred[4,8]{1,0:T(4,128)(4,1)S(1)}, u32[]{:S(2)}) copy-start(pred[4,8]{1,0:T(4,128)(4,1)S(1)} %get-tuple-element.9) | copy-start | bytes 100
  169.6 1.9 copy-start.1
  182.7 0.6 copy-start.3
  260.9 9.5 %copy-start.5 = (f32[4,8]{1,0:T(4,128)}, f32[4,8]{1,0:T(4,128)S(1)}, u32[]{:S(2)}) copy-start(f32[4,8]{1,0:T(4,128)S(1)} %get-tuple-element.5) | copy-start | bytes 388
  263.8 216.2 %reduce-scatter.2.cloned.1.call-start = ((), (), s32[]{:S(2)}) async-start(), calls=%async_computation.2 | async-start | bytes 7077888 | tf_op jit(solution)/shard_map/reduce_scatter | solution.py:61
  272.1 3.0 copy-start.8
  272.1 3.1 copy-start.9
  272.1 133.3 %copy-start.4 = (f32[4,2000]{1,0:T(4,128)S(1)}, f32[4,2000]{1,0:T(4,128)}, u32[]{:S(2)}) copy-start(f32[4,2000]{1,0:T(4,128)} %copy-done.3) | copy-start | bytes 96004
  411.7 2.9 copy-start.6
  414.6 2.8 copy-start.2
Sparse Core Ops, SparseCore 0:
  10.5 147.1 all-gather.2
  263.9 141.4 all-reduce.3
  433.5 46.4 reduce-scatter.1
where the time goes:
time: 487 us
  waiting for transfers between devices  322 us (66%)
  blocking collectives  69.3 us (14%)
  local copies, waits for them, and re-layouts  32.5 us (7%)
  matrix products  24.6 us (5%)
  other arithmetic  23.6 us (5%)
  between operations  14.5 us (3%)
    all_gather x1, waiting for transfers between devices, per_device(): head_full = lax.all_gather(head_weight, 'dp', axis=0, tiled=True)  144 us
    unnamed x4, waiting for transfers between devices  131 us
    reduce_scatter x1, waiting for transfers between devices, per_device(): lax.psum_scatter(lax.dot_general(logit_grad, head_full, (((1,), (1,)), ((...  46.6 us
    all_gather x1, blocking collectives, per_device(): gathered = lax.all_gather(passage_rep, 'dp', axis=0, tiled=True)  42.1 us
    psum x1, blocking collectives, per_device(): positive, negative = lax.psum((pos_part, neg_part), 'vocab')  27.3 us
    dot_general x1, matrix products, per_device(): lax.dot_general(logit_grad, head_full, (((1,), (1,)), ((), ())), preferre...  12.6 us
    dot_general x1, matrix products, per_device(): jnp.dot(hidden, head_full, preferred_element_type=jnp.float32)  12 us
  transfers between devices with their start and end apart: 3, of which 3 were waited for; matrix products, arithmetic and copies ran while one was open for 3% of the time, Pallas kernels for 0%

commit v1 on v0

--- a/solution.py
+++ b/solution.py
@@ -26,7 +26,9 @@
     query_count = neg_owner.shape[0]
     neg_count = neg_owner.shape[1]
     owners = lax.axis_size("dp")
-    head_full = lax.all_gather(head_weight, "dp", axis=0, tiled=True)
+    head_full = jnp.concatenate(
+        lax.all_to_all(jnp.stack([head_weight] * lax.axis_size("dp")), "dp", 0, 0), axis=0
+    )
     vocab_width = head_full.shape[1]
     logits = jnp.dot(hidden, head_full, preferred_element_type=jnp.float32) + head_bias[None, :]
     query_tokens = query_count * LQ

time: 487 us -> 749 us (1.54)
  waiting for transfers between devices: 322 us -> 563 us
  local copies, waits for them, and re-layouts: 32.5 us -> 45.6 us
  starting transfers between devices: 0.3 us -> 12.5 us
  other arithmetic: 23.6 us -> 11.8 us
    all_to_all x0 -> x1, waiting for transfers between devices: none -> 379 us  [per_device(): lax.all_to_all(jnp.stack([head_weight] * lax.axis_size('dp')), 'dp', 0, 0)]
    all_gather x1 -> x0, waiting for transfers between devices: 144 us -> none  [per_device(): head_full = lax.all_gather(head_weight, 'dp', axis=0, tiled=True)]
    all_to_all x0 -> x1, local copies, waits for them, and re-layouts: none -> 22.6 us  [per_device(): lax.all_to_all(jnp.stack([head_weight] * lax.axis_size('dp')), 'dp', 0, 0)]
    all_to_all x0 -> x1, starting transfers between devices: none -> 12.3 us  [per_device(): lax.all_to_all(jnp.stack([head_weight] * lax.axis_size('dp')), 'dp', 0, 0)]
    all_gather x1, blocking collectives: 42.1 us -> 52.2 us  [per_device(): gathered = lax.all_gather(passage_rep, 'dp', axis=0, tiled=True)]
    unnamed x4 -> x3, waiting for transfers between devices: 131 us -> 137 us
  transfers between devices with their start and end apart: 3 -> 3, of which waited for: 3 -> 3; matrix products, arithmetic and copies ran while one was open for 3% -> 1% of each run, Pallas kernels for 0% -> 0%
where the time goes in v1:
time: 749 us; the launch traced here: 748 us
  waiting for transfers between devices  563 us (75%)
  blocking collectives  76.3 us (10%)
  local copies, waits for them, and re-layouts  45.6 us (6%)
  matrix products  24.5 us (3%)
  between operations  14.9 us (2%)
  starting transfers between devices  12.5 us (2%)
  other arithmetic  11.8 us (2%)
    all_to_all x1, waiting for transfers between devices, per_device(): lax.all_to_all(jnp.stack([head_weight] * lax.axis_size('dp')), 'dp', 0, 0)  379 us
    unnamed x3, waiting for transfers between devices  137 us
    all_gather x1, blocking collectives, per_device(): gathered = lax.all_gather(passage_rep, 'dp', axis=0, tiled=True)  52.2 us
    reduce_scatter x1, waiting for transfers between devices, per_device(): lax.psum_scatter(lax.dot_general(logit_grad, head_full, (((1,), (1,)), ((...  46.7 us
    psum x1, blocking collectives, per_device(): positive, negative = lax.psum((pos_part, neg_part), 'vocab')  24.1 us
    all_to_all x1, local copies, waits for them, and re-layouts, per_device(): lax.all_to_all(jnp.stack([head_weight] * lax.axis_size('dp')), 'dp', 0, 0)  22.6 us
  transfers between devices with their start and end apart: 3, of which 3 were waited for; matrix products, arithmetic and copies ran while one was open for 1% of the time, Pallas kernels for 0%

profile of v1, /device:TPU:1, one launch (start us, length us, event | category | flops | bytes accessed | tf_op | source)
XLA Modules:
  0.0 748.5 jit_solution(14651119828422621183)
XLA Ops:
  7.2 7.3 stack.2
  14.5 12.3 %all-to-all-start = ((bf16[32,128,2000]{1,2,0:T(8,128)(2,1)}), bf16[32,128,2000]{1,2,0:T(8,128)(2,1)}, u32[]{:S(2)}, u32[]{:S(2)}) async-start(bf16[32,128,2000]{1,2,0:T(8,128)(2,1)} %stack.2), calls=%async_computation | async-start | bytes 32768000 | tf_op jit(solution)/shard_map/all_to_all | solution.py:30
  26.8 0.1 reshape.197
  26.9 0.1 reshape.210
  27.0 0.1 broadcast_in_dim.13
  27.1 0.2 fusion.21
  27.3 0.2 fusion.22
  27.5 0.1 fusion.19
  27.6 0.1 fusion.18
  27.6 378.6 %all-to-all-done = bf16[32,128,2000]{1,2,0:T(8,128)(2,1)} async-done(((bf16[32,128,2000]{1,2,0:T(8,128)(2,1)}), bf16[32,128,2000]{1,2,0:T(8,128)(2,1)}, u32[]{:S(2)}, u32[]{:S(2)}) %all-to-all-start) | async-done | bytes 16384032 | tf_op jit(solution)/shard_map/all_to_all | solution.py:30
  406.2 22.6 %copy.27 = bf16[32,128,2000]{2,1,0:T(8,128)(2,1)} copy(bf16[32,128,2000]{1,2,0:T(8,128)(2,1)} %all-to-all-done) | data formatting | bytes 32768000 | tf_op jit(solution)/shard_map/all_to_all | solution.py:30
  428.9 12.2 %convolution_add_fusion = f32[384,2000]{0,1:T(8,128)S(1)} fusion(bf16[384,4096]{1,0:T(8,128)(2,1)S(1)} %copy-done, bf16[4096,2000]{1,0:T(8,128)(2,1)} %bitcast.29, f32[2000]{0:T(1024)S(1)} %copy-done.12), kind=kOutput, calls=%fused_computation.4 | convolution fusion | flops 6292224000 | bytes 22609728 | tf_op jit(solution)/shard_map/dot_general | solution.py:33
  441.1 2.2 fusion.3
  443.4 1.4 fusion.10
  444.8 1.9 copy.29
  446.7 1.5 copy.28
  448.2 0.3 multiply_reduce_fusion
  448.5 0.2 multiply_reduce_fusion.1
  448.8 0.2 multiply_reduce_fusion.2
  449.0 52.2 %all-gather = f32[32,4,2000]{2,1,0:T(4,128)S(1)} all-gather(f32[1,4,2000]{2,1,0:T(4,128)S(1)} %multiply_bitcast_fusion), channel_id=1, replica_groups=mesh['dp'=32,'vocab'=8] {'dp'}, dimensions={0}, use_global_device_ids=true | all-gather | bytes 1056000 | tf_op jit(solution)/shard_map/all_gather | solution.py:41
  501.2 0.4 reshape.218
  501.6 0.7 gather_fusion
  502.2 0.2 fusion.13
  502.4 0.1 reduce_sum.80
  502.5 24.1 %all-reduce.1 = (f32[4,8]{1,0:T(4,128)S(1)}, f32[4]{0:T(128)S(1)}) all-reduce(f32[4,8]{1,0:T(4,128)S(1)} %reduce_sum.80, f32[4]{0:T(128)S(1)} %get-tuple-element.6), channel_id=1, replica_groups=mesh['dp'=32,'vocab'=8] {'vocab'}, use_global_device_ids=true, to_apply=%region_7.8 | all-reduce | flops 36 | bytes 288 | tf_op jit(solution)/shard_map/psum | solution.py:48
  526.6 0.2 fusion.26
  526.8 0.1 mul.151
  526.9 2.0 scatter_custom_fusion
  529.0 0.2 reduce-scatter.2.cloned.1.call-start
  529.2 0.1 reshape.198
  529.3 0.1 reshape.199
  529.4 0.6 dynamic-slice
  530.6 0.1 div.69
  530.7 1.3 copy.30
  532.0 0.2 div.72
  532.3 1.8 copy.33
  534.1 0.2 fusion.15
  534.3 137.5 %all-reduce.4.cloned.1.call-done = f32[128,2000]{1,0:T(8,128)} async-done(((f32[128,2000]{1,0:T(8,128)}), f32[128,2000]{1,0:T(8,128)}) %all-reduce.4.cloned.1.call-update) | async-done | bytes 1024016
  671.7 0.9 multiply_add_fusion
  672.6 0.1 mul.145
  672.7 1.3 copy.31
  674.0 1.6 mul.154
  675.6 3.0 copy.34
  678.7 2.2 divide_multiply_fusion.1
  680.9 0.5 copy-done.5
  681.5 1.1 divide_multiply_fusion
  682.6 12.3 %fusion.4 = f32[384,4096]{1,0:T(8,128)} fusion(bf16[4096,2000]{1,0:T(8,128)(2,1)} %bitcast.30, f32[256,2000]{0,1:T(8,128)S(1)} %divide_multiply_fusion, f32[128,2000]{0,1:T(8,128)S(1)} %divide_multiply_fusion.1, f32[384,2000]{0,1:T(8,128)S(1)} %copy-done.3), kind=kOutput, calls=%fused_computation.11 | convolution fusion | flops 6297600000 | bytes 28819456 | tf_op jit(solution)/shard_map/dot_general | solution.py:64
  694.9 46.7 %reduce-scatter.2.cloned.1.call-done = f32[48,4096]{1,0:T(8,128)} async-done(((f32[384,4096]{1,0:T(8,128)}), f32[48,4096]{1,0:T(8,128)}) %reduce-scatter.2.cloned.1.call-update) | async-done | bytes 786448 | tf_op jit(solution)/shard_map/reduce_scatter | solution.py:63
  (37 shorter events, 0.2 us)
Async XLA Ops:
  7.2 421.7 %copy-start = (bf16[384,4096]{1,0:T(8,128)(2,1)S(1)}, bf16[384,4096]{1,0:T(8,128)(2,1)}, u32[]{:S(2)}) copy-start(bf16[384,4096]{1,0:T(8,128)(2,1)} %param.8) | copy-start | bytes 9437188
  14.4 12.4 %copy-start.8 = (s32[4,8]{1,0:T(4,128)S(1)}, s32[4,8]{1,0:T(4,128)}, u32[]{:S(2)}) copy-start(s32[4,8]{1,0:T(4,128)} %param.14) | copy-start | bytes 388
  14.4 12.4 %copy-start.9 = (s32[4,8]{1,0:T(4,128)S(1)}, s32[4,8]{1,0:T(4,128)}, u32[]{:S(2)}) copy-start(s32[4,8]{1,0:T(4,128)} %param.13) | copy-start | bytes 388
  14.4 12.7 %copy-start.10 = (s32[4]{0:T(128)S(1)}, s32[4]{0:T(128)}, u32[]{:S(2)}) copy-start(s32[4]{0:T(128)} %param.12) | copy-start | bytes 52
  14.4 12.9 %copy-start.11 = (s32[4]{0:T(128)S(1)}, s32[4]{0:T(128)}, u32[]{:S(2)}) copy-start(s32[4]{0:T(128)} %param.11) | copy-start | bytes 52
  14.5 391.8 %all-to-all-start = ((bf16[32,128,2000]{1,2,0:T(8,128)(2,1)}), bf16[32,128,2000]{1,2,0:T(8,128)(2,1)}, u32[]{:S(2)}, u32[]{:S(2)}) async-start(bf16[32,128,2000]{1,2,0:T(8,128)(2,1)} %stack.2), calls=%async_computation | async-start | bytes 32768000 | tf_op jit(solution)/shard_map/all_to_all | solution.py:30
  26.8 645.0 %all-reduce.4.cloned.1.call-start = ((), (), s32[]{:S(2)}) async-start(), calls=%async_computation.3 | async-start | bytes 2097152
  27.6 401.2 %copy-start.12 = (f32[2000]{0:T(1024)S(1)}, f32[2000]{0:T(1024)}, u32[]{:S(2)}) copy-start(f32[2000]{0:T(1024)} %param.10) | copy-start | bytes 24004
  441.1 2.3 copy-start.2
  448.7 77.9 %copy-start.7 = (f32[4,8]{1,0:T(4,128)S(1)}, f32[4,8]{1,0:T(4,128)}, u32[]{:S(2)}) copy-start(f32[4,8]{1,0:T(4,128)} %param.15) | copy-start | bytes 388
  501.2 28.2 %copy-start.13 = (u32[256]{0:T(256)S(1)}, u32[256]{0:T(256)}, u32[]{:S(2)}) copy-start(u32[256]{0:T(256)} %constant.40) | copy-start | bytes 3076
  526.8 5.4 copy-start.6
  529.0 212.6 %reduce-scatter.2.cloned.1.call-start = ((), (), s32[]{:S(2)}) async-start(), calls=%async_computation.2 | async-start | bytes 7077888 | tf_op jit(solution)/shard_map/reduce_scatter | solution.py:63
  674.0 4.6 copy-start.3
  678.7 2.3 copy-start.4
  678.7 2.8 copy-start.5
  694.9 46.7 %copy-start.1 = (bf16[384,4096]{1,0:T(8,128)(2,1)S(1)}, bf16[384,4096]{1,0:T(8,128)(2,1)}, u32[]{:S(2)}) copy-start(bf16[384,4096]{1,0:T(8,128)(2,1)} %param.8) | copy-start | bytes 9437188
Sparse Core Ops, SparseCore 0:
  529.1 142.5 all-reduce.3
  695.1 46.4 reduce-scatter.1
